TPU v7x, 512 devices: a whole 4x4x16 slice. The times are simulated.
512 devices in a mesh: stn: 64 (over x, z_lo, y), chan: 8 (over z_hi, core).
Axes of the slice: x: 4, y: 4, z: 16 (z_hi: 4, z_lo: 4; z = z_hi * 4 + z_lo), core: 2. Of those that a mesh axis runs over, the one named last changes fastest.
Arguments:
- voltages: bfloat16 [512, 2, 143, 2048], P(('stn', 'chan')), may hold values from -6 to 6
- flags: float32 [256, 128], P('stn'), may hold values from 0 to 1, as said below
- station_row: int32 [256], P('stn'), may hold values from 0 to 255, each once
Outputs:
- visibility: bfloat16 [2048, 512, 512], P(('stn', 'chan'))
Inputs may be any that keep to these rules, and one draw needn't show every extreme that they name: `flags`: 0 marks a flagged spectrum of a station, 1 a fully usable one; some stations have 0 at all 128 spectra. `station_row`: every row pair is given to exactly one station.
All inputs are finite; a program needn't handle non-finite values.
Results may differ from a plain program's by a relative error of at most 0.006.
Values may be sent and summed in bfloat16 or wider, within the bound.
No kernel may reach another device: no remote copies, remote signals or barrier semaphores. Data moves between devices by JAX's collectives and lax.ppermute only.
A program may use at most 64 MiB of HBM per device.

v0:
```python
import math
import jax
import jax.numpy as jnp
from jax import lax
from jax.sharding import PartitionSpec as P


def filter_table(taps, lanes):
    total = taps * lanes
    places = jnp.arange(total, dtype=jnp.float32) + 0.5
    window = 0.5 - 0.5 * jnp.cos(2.0 * math.pi * places / total)
    return (jnp.sinc((places - 0.5 * total) / lanes) * window).reshape(taps, lanes)


def dft_tables(length):
    places = jnp.arange(length, dtype=jnp.int32)
    product = places[:, None] * places[None, :] % length
    angle = 2.0 * math.pi * product.astype(jnp.float32) / length
    return (jnp.cos(angle), jnp.sin(angle))


def twiddle_tables(outer, inner):
    product = (
        jnp.arange(outer, dtype=jnp.int32)[:, None]
        * jnp.arange(inner, dtype=jnp.int32)[None, :]
        % (outer * inner)
    )
    angle = 2.0 * math.pi * product.astype(jnp.float32) / (outer * inner)
    return (jnp.cos(angle), jnp.sin(angle))


def contract(form, left, right):
    return jnp.einsum(form, left, right, precision=lax.Precision.HIGHEST)


def channelize(voltages, spectra_count):
    inputs_here = voltages.shape[0]
    lanes = voltages.shape[3]
    taps = voltages.shape[2] - spectra_count + 1
    taps_table = filter_table(taps, lanes)
    real_acc = taps_table[0] * voltages[:, 0, 0:spectra_count, :].astype(jnp.float32)
    imag_acc = taps_table[0] * voltages[:, 1, 0:spectra_count, :].astype(jnp.float32)
    for tap_index in range(1, taps):
        real_acc = real_acc + taps_table[tap_index] * voltages[
            :, 0, tap_index : tap_index + spectra_count, :
        ].astype(jnp.float32)
        imag_acc = imag_acc + taps_table[tap_index] * voltages[
            :, 1, tap_index : tap_index + spectra_count, :
        ].astype(jnp.float32)
    inner = 128
    outer = lanes // inner
    real_grid = real_acc.reshape(inputs_here, spectra_count, outer, inner)
    imag_grid = imag_acc.reshape(inputs_here, spectra_count, outer, inner)
    cos_outer, sin_outer = dft_tables(outer)
    real_mid = contract("gtmn,mk->gtkn", real_grid, cos_outer) + contract(
        "gtmn,mk->gtkn", imag_grid, sin_outer
    )
    imag_mid = contract("gtmn,mk->gtkn", imag_grid, cos_outer) - contract(
        "gtmn,mk->gtkn", real_grid, sin_outer
    )
    cos_twist, sin_twist = twiddle_tables(outer, inner)
    real_twisted = real_mid * cos_twist + imag_mid * sin_twist
    imag_twisted = imag_mid * cos_twist - real_mid * sin_twist
    cos_inner, sin_inner = dft_tables(inner)
    real_out = contract("gtkn,nj->jkgt", real_twisted, cos_inner) + contract(
        "gtkn,nj->jkgt", imag_twisted, sin_inner
    )
    imag_out = contract("gtkn,nj->jkgt", imag_twisted, cos_inner) - contract(
        "gtkn,nj->jkgt", real_twisted, sin_inner
    )
    scale = 1.0 / math.sqrt(lanes)
    stacked = (jnp.stack([real_out, imag_out], axis=3) * scale).astype(jnp.bfloat16)
    return stacked.reshape(lanes, inputs_here, 2 * spectra_count)


def square_products(plain, turned):
    real_part = jnp.einsum("cat,cbt->cab", plain, plain, preferred_element_type=jnp.float32)
    imag_part = jnp.einsum("cat,cbt->cab", plain, turned, preferred_element_type=jnp.float32)
    return (real_part, imag_part)


def on_device(voltages, flags, station_row):
    spectra_count = flags.shape[1]
    inputs_here = voltages.shape[0]
    lanes = voltages.shape[3]
    stn_count = lax.axis_size("stn")
    chan_count = lax.axis_size("chan")
    per_device = lanes // (stn_count * chan_count)
    total_inputs = inputs_here * stn_count * chan_count
    flags_all, rows_all = (
        lax.all_gather(flags, "stn", axis=0, tiled=True),
        lax.all_gather(station_row, "stn", axis=0, tiled=True),
    )
    spectra = channelize(voltages, spectra_count)
    grouped = spectra.reshape(stn_count, chan_count, per_device, inputs_here, 2 * spectra_count)
    order = jnp.argsort(rows_all)
    rows = jnp.arange(total_inputs, dtype=jnp.int32)
    station_of = order[rows // 2]
    source = 2 * station_of + rows % 2
    moved = lax.all_to_all(
        lax.all_to_all(grouped, "stn", split_axis=0, concat_axis=3, tiled=True),
        "chan",
        split_axis=1,
        concat_axis=3,
        tiled=True,
    )
    from_stn = source // (chan_count * inputs_here)
    from_chan = source // inputs_here % chan_count
    within = source % inputs_here
    placed = from_chan * (stn_count * inputs_here) + from_stn * inputs_here + within
    arrived = moved.reshape(per_device, total_inputs, 2, spectra_count)
    weights = jnp.take(flags_all, station_of, axis=0)
    kept = (
        jnp.take(arrived, placed, axis=1).astype(jnp.float32) * weights[None, :, None, :]
    ).astype(jnp.bfloat16)
    plain = kept.reshape(per_device, total_inputs, 2 * spectra_count)
    turned = jnp.concatenate([-kept[:, :, 1], kept[:, :, 0]], axis=-1)
    count = jnp.dot(
        weights, weights.T, preferred_element_type=jnp.float32, precision=lax.Precision.HIGHEST
    )
    denom = jnp.maximum(count, 1.0)
    real_part, imag_part = square_products(plain, turned)
    below = rows[:, None] >= rows[None, :]
    return jnp.where(below[None], real_part / denom, imag_part / denom).astype(jnp.bfloat16)


def solution(mesh):
    placed = (P(("stn", "chan"), None, None, None), P("stn", None), P("stn"))
    return jax.shard_map(
        on_device,
        mesh=mesh,
        in_specs=placed,
        out_specs=P(("stn", "chan"), None, None),
        check_vma=False,
    )
```

profile of v0, /device:TPU:128, one launch (start us, length us, event | category | flops | bytes accessed | tf_op | source)
XLA Modules:
  0.0 374.9 jit_solution(11308704280490452566)
XLA Ops:
  0.0 0.6 fusion.19
  0.6 0.0 copy-start
  0.7 28.6 %slice_convert_fusion.15 = (f32[1,1,128,2048]{3,1,2,0:T(1,128)S(1)}, f32[1,1,128,2048]{3,1,2,0:T(1,128)S(1)}, f32[1,1,128,2048]{3,1,2,0:T(1,128)S(1)}, f32[1,1,1...) fusion(bf16[1,2,143,2048]{3,1,2,0:T(2,128)(2,1)} %param.3), kind=kLoop, calls=%fused_computation.41 | loop fusion | flops 4980736 | bytes 29884416 | tf_op jit(solution)/shard_map/convert_element_type | solution.py:42
  29.3 13.9 %slice_convert_fusion.1 = (f32[1,1,128,2048]{3,1,2,0:T(1,128)}, f32[1,1,128,2048]{3,1,2,0:T(1,128)}, f32[1,1,128,2048]{3,1,2,0:T(1,128)}, f32[1,1,128,2048]{3,1,...) fusion(bf16[1,2,143,2048]{3,1,2,0:T(2,128)(2,1)S(1)} %copy-done), kind=kLoop, calls=%fused_computation.27 | loop fusion | flops 3407872 | bytes 20447232 | tf_op jit(solution)/shard_map/convert_element_type | solution.py:49
  43.2 0.7 fusion.62
  43.9 0.7 fusion.114
  44.5 3.2 multiply_add_fusion
  47.8 1.0 fusion.52
  48.9 0.1 copy-done.1
  49.0 0.3 copy-done.2
  49.3 5.6 %multiply_add_fusion.1 = f32[128,16,128]{2,1,0:T(8,128)S(1)} fusion(f32[128,16,128]{2,1,0:T(8,128)S(1)} %bitcast.127, f32[128,16,128]{2,1,0:T(8,128)S(1)} %bitcast.128, f32[128,16,128]{2,1,0:T(8,128)S(1)} %bitcast.129, f32[128,16,128]{2,1,0:T(8,128)S(1)} %bitcast.130, f32[128,16,128]{2,1,0:T(8,128)S(1)} %bitcast.131, f32[128,16,128]{2,1,0:T(8,128)S(1)} %bitcast.149, ...), kind=kLoop, calls=%fused_computation.42 | loop fusion | flops 8126464 | bytes 17956864 | tf_op jit(solution)/shard_map/add | solution.py:44
  54.9 1.0 fusion.54
  56.0 0.0 copy-start.11
  56.0 1.1 fusion.3
  57.1 1.3 add_bitcast_fusion
  58.4 1.4 fusion.12
  59.9 1.4 fusion.8
  61.3 1.5 fusion.2
  62.8 1.7 fusion.1
  64.5 0.3 fusion
  64.8 1.1 copy.26
  65.9 0.7 convert_element_type.489
  66.6 41.1 %all_to_all.33 = bf16[64,8,4,1,256]{4,2,1,3,0:T(4,128)(2,1)S(1)} all-to-all(bf16[64,8,4,1,256]{4,2,1,3,0:T(4,128)(2,1)S(1)} %bitcast.147), channel_id=1, replica_groups=mesh['stn'=64,'chan'=8] {'stn'}, dimensions={0} | all-to-all | bytes 2097152 | tf_op jit(solution)/shard_map/all_to_all | solution.py:101
  107.8 0.2 copy.54
  108.0 0.0 copy-start.14
  108.0 1.4 copy.29
  109.4 11.3 %all-to-all-start.1 = ((bf16[1,8,4,64,256]{4,2,3,0,1:T(4,128)(2,1)}), bf16[1,8,4,64,256]{4,2,3,0,1:T(4,128)(2,1)S(1)}, u32[]{:S(2)}, u32[]{:S(2)}) async-start(bf16[1,8,4,64,256]{4,2,3,0,1:T(4,128)(2,1)} %copy.29), calls=%async_computation.1 | async-start | bytes 2097152 | tf_op jit(solution)/shard_map/all_to_all | solution.py:100
  120.6 1.3 dynamic-slice
  122.6 0.2 dynamic-update-slice
  122.8 40.8 %all-reduce = s32[256]{0:T(256)S(1)} all-reduce(s32[256]{0:T(256)S(1)} %dynamic-update-slice), channel_id=1, replica_groups=mesh['stn'=64,'chan'=8] {'stn'}, use_global_device_ids=true, to_apply=%add | all-reduce | flops 256 | bytes 2048
  163.6 3.1 sort.17
  166.8 3.5 gather_fusion
  170.3 192.1 %all-gather = f32[64,4,128]{2,1,0:T(4,128)S(1)} all-gather(f32[1,4,128]{2,1,0:T(4,128)S(1)} %bitcast.167), channel_id=1, replica_groups=mesh['stn'=64,'chan'=8] {'stn'}, dimensions={0}, use_global_device_ids=true | all-gather | bytes 133120 | tf_op jit(solution)/shard_map/all_gather | solution.py:91
  362.4 1.0 gather_fusion.2
  363.5 0.1 broadcast_select_fusion
  363.6 0.1 copy.34
  363.8 0.1 iota_compare_fusion
  363.9 2.0 convolution_maximum_fusion
  365.8 0.0 all-to-all-done.1
  365.8 2.6 gather_fusion.1
  368.5 1.0 copy.43
  369.4 0.3 multiply_convert_fusion
  369.8 0.1 mul.1704
  369.8 0.3 multiply_convert_fusion.1
  370.2 0.8 fusion.117
  371.0 0.1 fusion.14
  371.1 1.1 copy-done.3
  372.2 2.8 select_convert_fusion
  (32 shorter events, 0.1 us)
Async XLA Ops:
  0.6 28.7 %copy-start = (bf16[1,2,143,2048]{3,1,2,0:T(2,128)(2,1)S(1)}, bf16[1,2,143,2048]{3,1,2,0:T(2,128)(2,1)}, u32[]{:S(2)}) copy-start(bf16[1,2,143,2048]{3,1,2,0:T(2,128)(2,1)} %param.3) | copy-start | bytes 3514372
  47.7 1.2 copy-start.1
  47.7 1.5 copy-start.2
  47.8 1.5 copy-start.4
  47.8 1.5 copy-start.5
  47.8 1.5 copy-start.6
  47.8 1.5 copy-start.7
  47.8 1.5 copy-start.8
  47.8 1.5 copy-start.9
  47.8 1.5 copy-start.10
  56.0 1.1 copy-start.11
  56.0 1.1 copy-start.12
  108.0 14.6 %copy-start.14 = (s32[4]{0:T(128)S(1)}, s32[4]{0:T(128)}, u32[]{:S(2)}) copy-start(s32[4]{0:T(128)} %param.5) | copy-start | bytes 52
  109.4 60.9 %copy-start.13 = (f32[4,128]{1,0:T(4,128)S(1)}, f32[4,128]{1,0:T(4,128)}, u32[]{:S(2)}) copy-start(f32[4,128]{1,0:T(4,128)} %param.4) | copy-start | bytes 6148
  109.4 256.5 %all-to-all-start.1 = ((bf16[1,8,4,64,256]{4,2,3,0,1:T(4,128)(2,1)}), bf16[1,8,4,64,256]{4,2,3,0,1:T(4,128)(2,1)S(1)}, u32[]{:S(2)}, u32[]{:S(2)}) async-start(bf16[1,8,4,64,256]{4,2,3,0,1:T(4,128)(2,1)} %copy.29), calls=%async_computation.1 | async-start | bytes 2097152 | tf_op jit(solution)/shard_map/all_to_all | solution.py:100
  371.0 1.2 copy-start.3
where the time goes:
time: 375 us
  blocking collectives  274 us (73%)
  other arithmetic  57.2 us (15%)
  matrix products  16 us (4%)
  local copies, waits for them, and re-layouts  15.4 us (4%)
  starting transfers between devices  11.3 us (3%)
    all_gather x1, blocking collectives, on_device(): lax.all_gather(flags, 'stn', axis=0, tiled=True)  192 us
    all_to_all x1, blocking collectives, on_device(): lax.all_to_all(grouped, 'stn', split_axis=0, concat_axis=3, tiled=True)  41.1 us
    unnamed x1, blocking collectives  40.8 us
    convert_element_type x1, other arithmetic, channelize(): voltages[:, 1, 0:spectra_count, :].astype(jnp.float32)  28.6 us
    convert_element_type x1, other arithmetic, channelize(): imag_acc = imag_acc + taps_table[tap_index] * voltages[:, 1, tap_index:ta...  13.9 us
    all_to_all x1, starting transfers between devices, on_device(): lax.all_to_all(lax.all_to_all(grouped, 'stn', split_axis=0, concat_axis=3...  11.3 us
    dot_general x8, matrix products, contract(): return jnp.einsum(form, left, right, precision=lax.Precision.HIGHEST)  10.6 us
  transfers between devices with their start and end apart: 1, of which 0 were waited for; matrix products, arithmetic and copies ran while one was open for 3% of the time, Pallas kernels for 0%

commit v1 on v0

--- a/solution.py
+++ b/solution.py
@@ -87,8 +87,20 @@
     chan_count = lax.axis_size("chan")
     per_device = lanes // (stn_count * chan_count)
     total_inputs = inputs_here * stn_count * chan_count
+
+    def work_column(x0, device_axis, along_dim=0):
+        return jnp.concatenate(
+            jax.lax.all_to_all(
+                jnp.stack([x0] * jax.lax.axis_size(device_axis), axis=0),
+                axis_name=device_axis,
+                split_axis=0,
+                concat_axis=0,
+            ),
+            axis=along_dim,
+        )
+
     flags_all, rows_all = (
-        lax.all_gather(flags, "stn", axis=0, tiled=True),
+        work_column(flags, "stn"),
         lax.all_gather(station_row, "stn", axis=0, tiled=True),
     )
     spectra = channelize(voltages, spectra_count)

time: 375 us -> 209 us (0.56)
  the two profiles are of different devices: /device:TPU:128 before, /device:TPU:32 now
where the time goes in v1:
time: 209 us
  blocking collectives  89.7 us (43%)
  other arithmetic  57.2 us (27%)
  starting transfers between devices  20.5 us (10%)
  local copies, waits for them, and re-layouts  16.4 us (8%)
  matrix products  16 us (8%)
  waiting for transfers between devices  7.94 us (4%)
    unnamed x1, blocking collectives  52 us
    all_to_all x1, blocking collectives, on_device(): lax.all_to_all(grouped, 'stn', split_axis=0, concat_axis=3, tiled=True)  37.7 us
    convert_element_type x1, other arithmetic, channelize(): voltages[:, 1, 0:spectra_count, :].astype(jnp.float32)  28.6 us
    convert_element_type x1, other arithmetic, channelize(): imag_acc = imag_acc + taps_table[tap_index] * voltages[:, 1, tap_index:ta...  13.9 us
    all_to_all x1, starting transfers between devices, on_device(): lax.all_to_all(lax.all_to_all(grouped, 'stn', split_axis=0, concat_axis=3...  12.4 us
    dot_general x8, matrix products, contract(): return jnp.einsum(form, left, right, precision=lax.Precision.HIGHEST)  10.6 us
    all_to_all x1, starting transfers between devices, work_column(): jax.lax.all_to_all(jnp.stack([x0] * jax.lax.axis_size(device_axis), axis=...  8.08 us
    all_to_all x1, waiting for transfers between devices, work_column(): jax.lax.all_to_all(jnp.stack([x0] * jax.lax.axis_size(device_axis), axis=...  7.93 us
  transfers between devices with their start and end apart: 2, of which 1 were waited for; matrix products, arithmetic and copies ran while one was open for 6% of the time, Pallas kernels for 0%

profile of v1, /device:TPU:32, one launch (start us, length us, event | category | flops | bytes accessed | tf_op | source)
XLA Modules:
  0.0 208.8 jit_solution(8994661895441307875)
XLA Ops:
  0.0 0.6 fusion.19
  0.7 28.6 %slice_convert_fusion.15 = (f32[1,1,128,2048]{3,1,2,0:T(1,128)S(1)}, f32[1,1,128,2048]{3,1,2,0:T(1,128)S(1)}, f32[1,1,128,2048]{3,1,2,0:T(1,128)S(1)}, f32[1,1,1...) fusion(bf16[1,2,143,2048]{3,1,2,0:T(2,128)(2,1)} %param.3), kind=kLoop, calls=%fused_computation.41 | loop fusion | flops 4980736 | bytes 29884416 | tf_op jit(solution)/shard_map/convert_element_type | solution.py:42
  29.3 13.9 %slice_convert_fusion.1 = (f32[1,1,128,2048]{3,1,2,0:T(1,128)}, f32[1,1,128,2048]{3,1,2,0:T(1,128)}, f32[1,1,128,2048]{3,1,2,0:T(1,128)}, f32[1,1,128,2048]{3,1,...) fusion(bf16[1,2,143,2048]{3,1,2,0:T(2,128)(2,1)S(1)} %copy-done), kind=kLoop, calls=%fused_computation.27 | loop fusion | flops 3407872 | bytes 20447232 | tf_op jit(solution)/shard_map/convert_element_type | solution.py:49
  43.2 0.7 fusion.62
  43.9 0.7 fusion.114
  44.5 3.2 %multiply_add_fusion = f32[128,16,128]{2,1,0:T(8,128)S(1)} fusion(f32[128,16,128]{2,1,0:T(8,128)} %bitcast.160, f32[128,16,128]{2,1,0:T(8,128)} %bitcast.159, f32[128,16,128]{2,1,0:T(8,128)S(1)} %bitcast.132, f32[128,16,128]{2,1,0:T(8,128)S(1)} %bitcast.133, f32[128,16,128]{2,1,0:T(8,128)S(1)} %bitcast.134, f32[128,16,128]{2,1,0:T(8,128)S(1)} %bitcast.135, ...), kind=kLoop, calls=%fused_computation.25 | loop fusion | flops 8126464 | bytes 17956864 | tf_op jit(solution)/shard_map/add | solution.py:47
  47.8 1.0 fusion.52
  48.9 0.1 copy-done.1
  48.9 0.3 copy-done.2
  49.3 5.6 %multiply_add_fusion.1 = f32[128,16,128]{2,1,0:T(8,128)S(1)} fusion(f32[128,16,128]{2,1,0:T(8,128)S(1)} %bitcast.126, f32[128,16,128]{2,1,0:T(8,128)S(1)} %bitcast.127, f32[128,16,128]{2,1,0:T(8,128)S(1)} %bitcast.128, f32[128,16,128]{2,1,0:T(8,128)S(1)} %bitcast.129, f32[128,16,128]{2,1,0:T(8,128)S(1)} %bitcast.130, f32[128,16,128]{2,1,0:T(8,128)S(1)} %bitcast.148, ...), kind=kLoop, calls=%fused_computation.42 | loop fusion | flops 8126464 | bytes 17956864 | tf_op jit(solution)/shard_map/add | solution.py:44
  54.9 1.0 fusion.54
  56.0 1.1 fusion.3
  57.1 1.3 add_bitcast_fusion
  58.4 1.4 fusion.12
  59.8 1.4 fusion.8
  61.3 1.5 fusion.2
  62.8 1.7 fusion.1
  64.5 0.3 fusion
  64.8 1.1 copy.26
  65.9 0.0 copy-start.13
  65.9 0.7 convert_element_type.489
  66.6 37.7 %all_to_all.38 = bf16[64,8,4,1,256]{4,2,1,3,0:T(4,128)(2,1)S(1)} all-to-all(bf16[64,8,4,1,256]{4,2,1,3,0:T(4,128)(2,1)S(1)} %bitcast.146), channel_id=1, replica_groups=mesh['stn'=64,'chan'=8] {'stn'}, dimensions={0} | all-to-all | bytes 2097152 | tf_op jit(solution)/shard_map/all_to_all | solution.py:113
  104.3 0.7 stack.11
  104.9 8.1 %all-to-all-start.2 = ((f32[64,4,128]{2,1,0:T(4,128)}), f32[64,4,128]{2,1,0:T(4,128)S(1)}, u32[]{:S(2)}, u32[]{:S(2)}) async-start(f32[64,4,128]{2,1,0:T(4,128)} %stack.11), calls=%async_computation.2 | async-start | bytes 262144 | tf_op jit(solution)/shard_map/all_to_all | solution.py:93
  113.0 0.2 copy.54
  113.3 0.0 copy-start.14
  113.3 1.4 copy.29
  114.6 7.9 %all-to-all-done.2 = f32[64,4,128]{2,1,0:T(4,128)S(1)} async-done(((f32[64,4,128]{2,1,0:T(4,128)}), f32[64,4,128]{2,1,0:T(4,128)S(1)}, u32[]{:S(2)}, u32[]{:S(2)}) %all-to-all-start.2) | async-done | bytes 131104 | tf_op jit(solution)/shard_map/all_to_all | solution.py:93
  122.6 12.4 %all-to-all-start.1 = ((bf16[1,8,4,64,256]{4,2,3,0,1:T(4,128)(2,1)}), bf16[1,8,4,64,256]{4,2,3,0,1:T(4,128)(2,1)S(1)}, u32[]{:S(2)}, u32[]{:S(2)}) async-start(bf16[1,8,4,64,256]{4,2,3,0,1:T(4,128)(2,1)} %copy.29), calls=%async_computation.1 | async-start | bytes 2097152 | tf_op jit(solution)/shard_map/all_to_all | solution.py:112
  135.0 1.3 dynamic-slice
  136.9 0.2 dynamic-update-slice
  137.2 52.0 %all-reduce = s32[256]{0:T(256)S(1)} all-reduce(s32[256]{0:T(256)S(1)} %dynamic-update-slice), channel_id=1, replica_groups=mesh['stn'=64,'chan'=8] {'stn'}, use_global_device_ids=true, to_apply=%add | all-reduce | flops 256 | bytes 2048
  189.2 3.2 %sort.17 = (s32[256]{0:T(256)}, s32[256]{0:T(256)S(1)}) sort(s32[256]{0:T(256)S(1)} %all-reduce, s32[256]{0:T(256)S(1)} %iota.415), dimensions={0}, to_apply=%region_0.1 | sort | flops 2048 | bytes 4096 | tf_op jit(solution)/shard_map/jit(argsort)/sort | solution.py:108
  192.4 3.8 %gather_fusion = s32[512]{0:T(512)S(1)} fusion(s32[256]{0:T(256)S(1)} %get-tuple-element.6, s32[1024]{0:T(1024)S(1)} %pad_clamp_fusion.2), kind=kCustom, calls=%fused_computation | custom fusion | bytes 6144 | tf_op jit(solution)/shard_map/gather | solution.py:110
  196.2 0.1 iota_compare_fusion
  196.4 1.0 gather_fusion.2
  197.4 0.1 broadcast_select_fusion
  197.5 0.1 copy.34
  197.7 2.0 convolution_maximum_fusion
  199.6 2.6 %gather_fusion.1 = bf16[512,4,2,128]{3,1,2,0:T(4,128)(2,1)S(1)} fusion(bf16[4,512,2,128]{3,0,2,1:T(4,128)(2,1)S(1)} %bitcast.145, s32[1024]{0:T(1024)S(1)} %pad_clamp_fusion.1), kind=kCustom, calls=%fused_computation.1 | custom fusion | bytes 2099200 | tf_op jit(solution)/shard_map/jit(_take)/gather | solution.py:126
  202.3 1.0 copy.43
  203.2 0.3 multiply_convert_fusion
  203.6 0.1 mul.1704
  203.7 0.3 multiply_convert_fusion.1
  204.0 0.8 fusion.117
  204.8 0.1 fusion.14
  204.9 1.1 copy-done.3
  206.0 2.8 %select_convert_fusion = bf16[4,512,512]{2,1,0:T(8,128)(2,1)} fusion(f32[4,512,512]{2,1,0:T(8,128)S(1)} %fusion.117, f32[512,512]{1,0:T(8,128)S(1)} %copy-done.3, pred[512,512]{1,0:T(8,128)(4,1)S(1)} %iota_compare_fusion, bf16[4,512,256]{1,2,0:T(8,128)(2,1)S(1)} %multiply_convert_fusion.1, bf16[4,512,128]{2,1,0:T(8,128)(2,1)S(1)} %get-tuple-element.42, ...), kind=kOutput, calls=%fused_computation.3 | convolution fusion | flops 543162368 | bytes 9699328 | tf_op jit(solution)/shard_map/cat,cbt->cab/dot_general | solution.py:78
  (34 shorter events, 0.1 us)
Async XLA Ops:
  0.6 28.7 %copy-start = (bf16[1,2,143,2048]{3,1,2,0:T(2,128)(2,1)S(1)}, bf16[1,2,143,2048]{3,1,2,0:T(2,128)(2,1)}, u32[]{:S(2)}) copy-start(bf16[1,2,143,2048]{3,1,2,0:T(2,128)(2,1)} %param.3) | copy-start | bytes 3514372
  47.7 1.2 copy-start.1
  47.7 1.5 copy-start.2
  47.7 1.5 copy-start.4
  47.7 1.5 copy-start.5
  47.8 1.5 copy-start.6
  47.8 1.5 copy-start.7
  47.8 1.5 copy-start.8
  47.8 1.5 copy-start.9
  47.8 1.5 copy-start.10
  55.9 1.1 copy-start.11
  55.9 1.1 copy-start.12
  65.9 38.4 %copy-start.13 = (f32[4,128]{1,0:T(4,128)S(1)}, f32[4,128]{1,0:T(4,128)}, u32[]{:S(2)}) copy-start(f32[4,128]{1,0:T(4,128)} %param.4) | copy-start | bytes 6148
  104.9 17.6 %all-to-all-start.2 = ((f32[64,4,128]{2,1,0:T(4,128)}), f32[64,4,128]{2,1,0:T(4,128)S(1)}, u32[]{:S(2)}, u32[]{:S(2)}) async-start(f32[64,4,128]{2,1,0:T(4,128)} %stack.11), calls=%async_computation.2 | async-start | bytes 262144 | tf_op jit(solution)/shard_map/all_to_all | solution.py:93
  113.3 23.7 %copy-start.14 = (s32[4]{0:T(128)S(1)}, s32[4]{0:T(128)}, u32[]{:S(2)}) copy-start(s32[4]{0:T(128)} %param.5) | copy-start | bytes 52
  122.6 77.1 %all-to-all-start.1 = ((bf16[1,8,4,64,256]{4,2,3,0,1:T(4,128)(2,1)}), bf16[1,8,4,64,256]{4,2,3,0,1:T(4,128)(2,1)S(1)}, u32[]{:S(2)}, u32[]{:S(2)}) async-start(bf16[1,8,4,64,256]{4,2,3,0,1:T(4,128)(2,1)} %copy.29), calls=%async_computation.1 | async-start | bytes 2097152 | tf_op jit(solution)/shard_map/all_to_all | solution.py:112
  204.8 1.2 copy-start.3
